TPU v7x, 32 devices: a whole 2x2x4 slice. The times are simulated.
32 devices in a mesh: rep: 4 (over z), dp: 2 (over y), cp: 4 (over x, core).
Axes of the slice: x: 2, y: 2, z: 4, core: 2. Of those that a mesh axis runs over, the one named last changes fastest.
Arguments:
- block_in: bfloat16 [8, 1024, 2048], P(('rep', 'dp'), 'cp'), may hold values from -6 to 6
- positions: int32 [8, 1024], P(('rep', 'dp')), may hold values from 0 to 1023, as said below
- norm_attn: bfloat16 [2048], P(('dp', 'cp')), may hold values from 0.5 to 1.5
- w_query: bfloat16 [2048, 2048], P(('dp', 'cp')), may hold values from -0.125 to 0.125
- key_weight: bfloat16 [2048, 512], P(('dp', 'cp')), may hold values from -0.125 to 0.125
- w_value: bfloat16 [2048, 512], P(('dp', 'cp')), may hold values from -0.125 to 0.125
- w_out: bfloat16 [2048, 2048], P(('dp', 'cp')), may hold values from -2 to 2
- norm_ffn: bfloat16 [2048], P(('dp', 'cp')), may hold values from 0.5 to 1.5
- w_gate: bfloat16 [2048, 8192], P(('dp', 'cp')), may hold values from -0.125 to 0.125
- w_up: bfloat16 [2048, 8192], P(('dp', 'cp')), may hold values from -0.125 to 0.125
- w_down: bfloat16 [8192, 2048], P(('dp', 'cp')), may hold values from -0.0625 to 0.0625
- cotangent: bfloat16 [8, 1024, 2048], P(('rep', 'dp'), 'cp'), may hold values from -6 to 6
Outputs:
- block_out: bfloat16 [8, 1024, 2048], P(('rep', 'dp'), 'cp')
- input_grad: bfloat16 [8, 1024, 2048], P(('rep', 'dp'), 'cp')
- norm_attn_grad: float32 [2048], P(('dp', 'cp'))
- w_query_grad: float32 [2048, 2048], P(('dp', 'cp'))
- w_key_grad: float32 [2048, 512], P(('dp', 'cp'))
- w_value_grad: float32 [2048, 512], P(('dp', 'cp'))
- w_out_grad: float32 [2048, 2048], P(('dp', 'cp'))
- norm_ffn_grad: float32 [2048], P(('dp', 'cp'))
- w_gate_grad: float32 [2048, 8192], P(('dp', 'cp'))
- w_up_grad: float32 [2048, 8192], P(('dp', 'cp'))
- w_down_grad: float32 [8192, 2048], P(('dp', 'cp'))
Inputs may be any that keep to these rules, and one draw needn't show every extreme that they name: Each row of positions is a permutation of 0 to 1023 made of runs of 64 consecutive positions that start at multiples of 64.
All inputs are finite; a program needn't handle non-finite values.
Results may differ from a plain program's by a relative error of at most 0.02.
Values may be sent and summed in bfloat16 or wider, within the bound.
A program may use at most 512 MiB of HBM per device.

v0:
```python
import jax
import jax.numpy as jnp
from jax import lax
from jax.sharding import PartitionSpec as P

QUERY_HEADS = 32
KEY_VALUE_HEADS = 8
HEAD_SIZE = 64
QW = 2048
KEY_FEATURES = 512


NORM_EPS = 1e-05
ROPE_THETA = 500000.0
NEG_FILL = -1e30


def matrix_product(left_rows, right_rows):
    return jnp.dot(left_rows, right_rows, preferred_element_type=jnp.float32)


def dot_back(left_rows, right_rows):
    return lax.dot_general(
        left_rows, right_rows, (((1,), (1,)), ((), ())), preferred_element_type=jnp.float32
    )


def dot_inner(left_rows, right_rows):
    return lax.dot_general(
        left_rows, right_rows, (((0,), (0,)), ((), ())), preferred_element_type=jnp.float32
    )


def angle_tables(position_rows):
    inverse_freq = ROPE_THETA ** (-jnp.arange(HEAD_SIZE // 2, dtype=jnp.float32) * 2.0 / HEAD_SIZE)
    angle_table = position_rows.astype(jnp.float32)[:, None] * inverse_freq[None, :]
    return (jnp.cos(angle_table), jnp.sin(angle_table))


def apply_rotary(field_in, cosine_table, sine_values, heads_count):
    shaped = field_in.reshape(field_in.shape[0], heads_count, HEAD_SIZE)
    leading = shaped[..., : HEAD_SIZE // 2]
    trailing = shaped[..., HEAD_SIZE // 2 :]
    cos_part = cosine_table[:, None, :]
    sin_part = sine_values[:, None, :]
    joined = jnp.concatenate(
        [leading * cos_part - trailing * sin_part, trailing * cos_part + leading * sin_part],
        axis=-1,
    )
    return joined.reshape(field_in.shape)


def rms_apply(field_in, gain_vec):
    inverse = lax.rsqrt(jnp.mean(field_in * field_in, axis=-1, keepdims=True) + NORM_EPS)
    return (field_in * inverse * gain_vec, inverse)


def rms_back(field_in, inverse, gain_vec, grad_rows):
    scaled = grad_rows * gain_vec
    gain_grad = jnp.sum(grad_rows * field_in * inverse, axis=0)
    row_inner = jnp.mean(scaled * field_in, axis=-1, keepdims=True)
    return (inverse * scaled - field_in * inverse * inverse * inverse * row_inner, gain_grad)


def head_scores(q_one, k_one, allowed):
    scores = jnp.einsum(
        "btgd,bld->bgtl", q_one, k_one, preferred_element_type=jnp.float32
    ) * HEAD_SIZE ** (-0.5)
    return jnp.where(allowed[:, None], scores, NEG_FILL)


def attention_forward(
    query_row_block, key_gathered_all, value_gathered_all, allowed, sequence_count, token_count
):
    query_groups = QUERY_HEADS // KEY_VALUE_HEADS
    query_head_rows = jnp.moveaxis(
        query_row_block.reshape(
            sequence_count, token_count, KEY_VALUE_HEADS, query_groups, HEAD_SIZE
        ),
        2,
        0,
    )
    key_head_rows = jnp.moveaxis(
        key_gathered_all.reshape(sequence_count, -1, KEY_VALUE_HEADS, HEAD_SIZE), 2, 0
    )
    value_head_rows = jnp.moveaxis(
        value_gathered_all.reshape(sequence_count, -1, KEY_VALUE_HEADS, HEAD_SIZE), 2, 0
    )

    def one_head(operands):
        q_one, k_one, v_one = operands
        scores = head_scores(q_one, k_one, allowed)
        row_max = jnp.max(scores, axis=-1, keepdims=True)
        weights = jnp.exp(scores - row_max)
        row_total = jnp.sum(weights, axis=-1, keepdims=True)
        soft_probs = (weights / row_total).astype(jnp.bfloat16)
        head_out = jnp.einsum(
            "bgtl,bld->btgd", soft_probs, v_one, preferred_element_type=jnp.float32
        )
        return (head_out, row_max + jnp.log(row_total))

    outputs, log_total = lax.map(one_head, (query_head_rows, key_head_rows, value_head_rows))
    return (jnp.moveaxis(outputs, 0, 2).reshape(sequence_count * token_count, QW), log_total)


def attention_backward(
    query_row_block,
    key_gathered_all,
    value_gathered_all,
    allowed,
    log_total,
    attended_gradient,
    sequence_count,
    token_count,
):
    query_groups = QUERY_HEADS // KEY_VALUE_HEADS
    query_head_rows = jnp.moveaxis(
        query_row_block.reshape(
            sequence_count, token_count, KEY_VALUE_HEADS, query_groups, HEAD_SIZE
        ),
        2,
        0,
    )
    key_head_rows = jnp.moveaxis(
        key_gathered_all.reshape(sequence_count, -1, KEY_VALUE_HEADS, HEAD_SIZE), 2, 0
    )
    value_head_rows = jnp.moveaxis(
        value_gathered_all.reshape(sequence_count, -1, KEY_VALUE_HEADS, HEAD_SIZE), 2, 0
    )
    heads_gradient = jnp.moveaxis(
        attended_gradient.reshape(
            sequence_count, token_count, KEY_VALUE_HEADS, query_groups, HEAD_SIZE
        ),
        2,
        0,
    )

    def one_head(operands):
        q_one, k_one, v_one, lse_one, grad_one = operands
        soft_probs = jnp.exp(head_scores(q_one, k_one, allowed) - lse_one)
        probs_low = soft_probs.astype(jnp.bfloat16)
        prob_grad = jnp.einsum(
            "btgd,bld->bgtl", grad_one, v_one, preferred_element_type=jnp.float32
        )
        row_inner = jnp.sum(soft_probs * prob_grad, axis=-1, keepdims=True)
        score_low = (soft_probs * (prob_grad - row_inner)).astype(jnp.bfloat16)
        q_grad = jnp.einsum(
            "bgtl,bld->btgd", score_low, k_one, preferred_element_type=jnp.float32
        ) * HEAD_SIZE ** (-0.5)
        k_grad = jnp.einsum(
            "bgtl,btgd->bld", score_low, q_one, preferred_element_type=jnp.float32
        ) * HEAD_SIZE ** (-0.5)
        v_grad = jnp.einsum(
            "bgtl,btgd->bld", probs_low, grad_one, preferred_element_type=jnp.float32
        )
        return (q_grad, k_grad, v_grad)

    q_grads, k_grads, v_grads = lax.map(
        one_head, (query_head_rows, key_head_rows, value_head_rows, log_total, heads_gradient)
    )
    query_grad = jnp.moveaxis(q_grads, 0, 2).reshape(sequence_count * token_count, QW)
    key_part = jnp.moveaxis(k_grads, 0, 2).reshape(sequence_count, -1, KEY_FEATURES)
    value_part = jnp.moveaxis(v_grads, 0, 2).reshape(sequence_count, -1, KEY_FEATURES)
    return (query_grad, key_part, value_part)


def scatter_rows(left_rows, right_rows):
    return lax.psum_scatter(
        dot_inner(left_rows, right_rows).astype(jnp.bfloat16),
        ("dp", "cp"),
        scatter_dimension=0,
        tiled=True,
    ).astype(jnp.float32)


def per_device(
    block_in,
    positions,
    norm_attn,
    w_query,
    key_weight,
    w_value,
    w_out,
    norm_ffn,
    w_gate,
    w_up,
    w_down,
    cotangent,
):
    sequence_count, token_count, model_width = block_in.shape
    in_rows = block_in.astype(jnp.float32).reshape(sequence_count * token_count, model_width)
    cp_rank = lax.axis_index("cp")
    query_pos = lax.dynamic_slice_in_dim(positions, cp_rank * token_count, token_count, 1)
    cosine_table, sine_values = angle_tables(query_pos.reshape(-1))
    allowed = positions[:, None, :] <= query_pos[:, :, None]
    g_query, key_gradient, g_value, g_out, gain_attn = (
        lax.all_gather(w_query, ("dp", "cp"), axis=0, tiled=True),
        lax.all_gather(key_weight, ("dp", "cp"), axis=0, tiled=True),
        lax.all_gather(w_value, ("dp", "cp"), axis=0, tiled=True),
        lax.all_gather(w_out, ("dp", "cp"), axis=0, tiled=True),
        lax.all_gather(norm_attn, ("dp", "cp"), axis=0, tiled=True),
    )
    normalized, inverse_attn = rms_apply(in_rows, gain_attn)
    normalized_reduced = normalized.astype(jnp.bfloat16)
    query_row_block = apply_rotary(
        matrix_product(normalized_reduced, g_query), cosine_table, sine_values, QUERY_HEADS
    ).astype(jnp.bfloat16)
    key_row_block = apply_rotary(
        matrix_product(normalized_reduced, key_gradient), cosine_table, sine_values, KEY_VALUE_HEADS
    ).astype(jnp.bfloat16)
    value_rows = matrix_product(normalized_reduced, g_value).astype(jnp.bfloat16)
    key_gathered_all, value_gathered_all = (
        lax.all_gather(
            key_row_block.reshape(sequence_count, token_count, KEY_FEATURES),
            "cp",
            axis=1,
            tiled=True,
        ),
        lax.all_gather(
            value_rows.reshape(sequence_count, token_count, KEY_FEATURES), "cp", axis=1, tiled=True
        ),
    )
    attended, log_total = attention_forward(
        query_row_block, key_gathered_all, value_gathered_all, allowed, sequence_count, token_count
    )
    attended_low = attended.astype(jnp.bfloat16)
    mid_rows = in_rows + matrix_product(attended_low, g_out)
    g_gate, g_up, g_down, gain_ffn = (
        lax.all_gather(w_gate, ("dp", "cp"), axis=0, tiled=True),
        lax.all_gather(w_up, ("dp", "cp"), axis=0, tiled=True),
        lax.all_gather(w_down, ("dp", "cp"), axis=0, tiled=True),
        lax.all_gather(norm_ffn, ("dp", "cp"), axis=0, tiled=True),
    )
    normed_ffn, inverse_ffn = rms_apply(mid_rows, gain_ffn)
    ffn_low = normed_ffn.astype(jnp.bfloat16)
    gate_proj = matrix_product(ffn_low, g_gate)
    up_proj = matrix_product(ffn_low, g_up)
    gate_sigmoid = jax.nn.sigmoid(gate_proj)
    hidden = (gate_proj * gate_sigmoid * up_proj).astype(jnp.bfloat16)
    result = mid_rows + matrix_product(hidden, g_down)
    block_out = result.astype(jnp.bfloat16).reshape(block_in.shape)
    back_gate, back_up, back_down, back_gain_ffn = (
        lax.all_gather(w_gate, ("dp", "cp"), axis=0, tiled=True),
        lax.all_gather(w_up, ("dp", "cp"), axis=0, tiled=True),
        lax.all_gather(w_down, ("dp", "cp"), axis=0, tiled=True),
        lax.all_gather(norm_ffn, ("dp", "cp"), axis=0, tiled=True),
    )
    grad_out = cotangent.reshape(sequence_count * token_count, model_width)
    down_grad = scatter_rows(hidden, grad_out)
    hidden_grad = dot_back(grad_out, back_down)
    silu_grad = gate_sigmoid * (1.0 + gate_proj * (1.0 - gate_sigmoid))
    gate_low = (hidden_grad * up_proj * silu_grad).astype(jnp.bfloat16)
    up_low = (hidden_grad * gate_proj * gate_sigmoid).astype(jnp.bfloat16)
    gate_grad = scatter_rows(ffn_low, gate_low)
    up_grad = scatter_rows(ffn_low, up_low)
    ffn_in_grad = dot_back(gate_low, back_gate) + dot_back(up_low, back_up)
    mid_part, gain_ffn_grad = rms_back(mid_rows, inverse_ffn, back_gain_ffn, ffn_in_grad)
    mid_grad = grad_out.astype(jnp.float32) + mid_part
    branch_low = mid_grad.astype(jnp.bfloat16)
    back_query, back_key, back_value, back_out, back_gain_attn = (
        lax.all_gather(w_query, ("dp", "cp"), axis=0, tiled=True),
        lax.all_gather(key_weight, ("dp", "cp"), axis=0, tiled=True),
        lax.all_gather(w_value, ("dp", "cp"), axis=0, tiled=True),
        lax.all_gather(w_out, ("dp", "cp"), axis=0, tiled=True),
        lax.all_gather(norm_attn, ("dp", "cp"), axis=0, tiled=True),
    )
    out_proj_grad = dot_inner(attended_low, branch_low)
    attended_gradient = dot_back(branch_low, back_out).astype(jnp.bfloat16)
    query_grad, key_part, value_part = attention_backward(
        query_row_block,
        key_gathered_all,
        value_gathered_all,
        allowed,
        log_total,
        attended_gradient,
        sequence_count,
        token_count,
    )
    key_local, value_own = (
        lax.psum_scatter(
            key_part.astype(jnp.bfloat16), "cp", scatter_dimension=1, tiled=True
        ).astype(jnp.float32),
        lax.psum_scatter(
            value_part.astype(jnp.bfloat16), "cp", scatter_dimension=1, tiled=True
        ).astype(jnp.float32),
    )
    query_low = apply_rotary(query_grad, cosine_table, -sine_values, QUERY_HEADS).astype(
        jnp.bfloat16
    )
    key_reduced = apply_rotary(
        key_local.reshape(sequence_count * token_count, KEY_FEATURES),
        cosine_table,
        -sine_values,
        KEY_VALUE_HEADS,
    ).astype(jnp.bfloat16)
    value_low = value_own.reshape(sequence_count * token_count, KEY_FEATURES).astype(jnp.bfloat16)
    query_w_grad = dot_inner(normalized_reduced, query_low)
    key_w_grad = dot_inner(normalized_reduced, key_reduced)
    value_w_grad = dot_inner(normalized_reduced, value_low)
    normed_grad = (
        dot_back(query_low, back_query)
        + dot_back(key_reduced, back_key)
        + dot_back(value_low, back_value)
    )
    in_part, gain_attn_grad = rms_back(in_rows, inverse_attn, back_gain_attn, normed_grad)
    input_grad = (mid_grad + in_part).astype(jnp.bfloat16).reshape(block_in.shape)
    query_share, key_share, value_share, out_share, gain_attn_share, gain_ffn_share = (
        lax.psum_scatter(
            query_w_grad.astype(jnp.bfloat16), ("dp", "cp"), scatter_dimension=0, tiled=True
        ).astype(jnp.float32),
        lax.psum_scatter(
            key_w_grad.astype(jnp.bfloat16), ("dp", "cp"), scatter_dimension=0, tiled=True
        ).astype(jnp.float32),
        lax.psum_scatter(
            value_w_grad.astype(jnp.bfloat16), ("dp", "cp"), scatter_dimension=0, tiled=True
        ).astype(jnp.float32),
        lax.psum_scatter(
            out_proj_grad.astype(jnp.bfloat16), ("dp", "cp"), scatter_dimension=0, tiled=True
        ).astype(jnp.float32),
        lax.psum_scatter(
            gain_attn_grad.astype(jnp.bfloat16), ("dp", "cp"), scatter_dimension=0, tiled=True
        ).astype(jnp.float32),
        lax.psum_scatter(
            gain_ffn_grad.astype(jnp.bfloat16), ("dp", "cp"), scatter_dimension=0, tiled=True
        ).astype(jnp.float32),
    )
    summed = (
        lax.psum(gain_attn_share.astype(jnp.bfloat16), "rep").astype(jnp.float32),
        lax.psum(query_share.astype(jnp.bfloat16), "rep").astype(jnp.float32),
        lax.psum(key_share.astype(jnp.bfloat16), "rep").astype(jnp.float32),
        lax.psum(value_share.astype(jnp.bfloat16), "rep").astype(jnp.float32),
        lax.psum(out_share.astype(jnp.bfloat16), "rep").astype(jnp.float32),
        lax.psum(gain_ffn_share.astype(jnp.bfloat16), "rep").astype(jnp.float32),
        lax.psum(gate_grad.astype(jnp.bfloat16), "rep").astype(jnp.float32),
        lax.psum(up_grad.astype(jnp.bfloat16), "rep").astype(jnp.float32),
        lax.psum(down_grad.astype(jnp.bfloat16), "rep").astype(jnp.float32),
    )
    return (
        block_out,
        input_grad,
        summed[0],
        summed[1],
        summed[2],
        summed[3],
        summed[4],
        summed[5],
        summed[6],
        summed[7],
        summed[8],
    )


def solution(mesh):
    return jax.shard_map(
        per_device,
        mesh=mesh,
        in_specs=(
            P(("rep", "dp"), "cp", None),
            P(("rep", "dp"), None),
            P(("dp", "cp")),
            P(("dp", "cp"), None),
            P(("dp", "cp"), None),
            P(("dp", "cp"), None),
            P(("dp", "cp"), None),
            P(("dp", "cp")),
            P(("dp", "cp"), None),
            P(("dp", "cp"), None),
            P(("dp", "cp"), None),
            P(("rep", "dp"), "cp", None),
        ),
        out_specs=(
            P(("rep", "dp"), "cp", None),
            P(("rep", "dp"), "cp", None),
            P(("dp", "cp")),
            P(("dp", "cp"), None),
            P(("dp", "cp"), None),
            P(("dp", "cp"), None),
            P(("dp", "cp"), None),
            P(("dp", "cp")),
            P(("dp", "cp"), None),
            P(("dp", "cp"), None),
            P(("dp", "cp"), None),
        ),
        check_vma=False,
    )
```

profile of v0, /device:TPU:0, one launch (start us, length us, event | category | flops | bytes accessed | tf_op | source)
XLA Modules:
  0.0 2330.4 jit_solution(2910926258638203179)
XLA Ops:
  21.4 19.1 all-gather.13.cloned.1.call-done
  45.4 24.7 %all-gather.15.cloned.1.call-done = bf16[2048,512]{1,0:T(8,128)(2,1)} async-done(((bf16[256,512]{1,0:T(8,128)(2,1)}), bf16[2048,512]{1,0:T(8,128)(2,1)}) %all-gather.15.cloned.1.call-update) | async-done | bytes 2097168 | tf_op jit(solution)/shard_map/all_gather | solution.py:198
  91.4 53.6 %all-gather.19.cloned.1.call-done = bf16[2048,2048]{1,0:T(8,128)(2,1)} async-done(((bf16[256,2048]{1,0:T(8,128)(2,1)}), bf16[2048,2048]{1,0:T(8,128)(2,1)}) %all-gather.19.cloned.1.call-update) | async-done | bytes 8388624 | tf_op jit(solution)/shard_map/all_gather | solution.py:197
  163.9 40.6 %while.30 = (s32[]{:T(128)}, bf16[8,1,256,4,64]{2,4,3,1,0:T(8,128)(2,1)S(1)}, f32[8,1,4,256,1]{3,2,4,1,0:T(4,128)S(1)}, bf16[8,1,1024,64]{2,3,1,0:T(8,128)(2,1)}...) while((s32[]{:T(128)}, ...), condition=%wide.region_4.5_spmd.clone.clone, body=%wide.region_1.4_spmd.clone.sunk.clone | while | flops 281279488 | bytes 14326881 | solution.py:102
  226.4 156.1 %all-gather.23.cloned.1.call-done = bf16[2048,8192]{1,0:T(8,128)(2,1)} async-done(((bf16[256,8192]{1,0:T(8,128)(2,1)}), bf16[2048,8192]{1,0:T(8,128)(2,1)}) %all-gather.23.cloned.1.call-update) | async-done | bytes 33554448 | tf_op jit(solution)/shard_map/all_gather | solution.py:229
  382.5 20.2 fusion.115
  402.7 142.4 %all-gather.25.cloned.1.call-done = bf16[2048,8192]{1,0:T(8,128)(2,1)} async-done(((bf16[256,8192]{1,0:T(8,128)(2,1)}), bf16[2048,8192]{1,0:T(8,128)(2,1)}) %all-gather.25.cloned.1.call-update) | async-done | bytes 33554448 | tf_op jit(solution)/shard_map/all_gather | solution.py:230
  545.1 20.5 fusion.116
  565.6 142.1 %all-gather.27.cloned.1.call-done = bf16[8192,2048]{1,0:T(8,128)(2,1)} async-done(((bf16[1024,2048]{1,0:T(8,128)(2,1)}), bf16[8192,2048]{1,0:T(8,128)(2,1)}) %all-gather.27.cloned.1.call-update) | async-done | bytes 33554448 | tf_op jit(solution)/shard_map/all_gather | solution.py:231
  707.7 23.9 %multiply_convert_fusion = (bf16[256,8192]{1,0:T(8,128)(2,1)}, bf16[256,8192]{1,0:T(8,128)(2,1)}, bf16[256,8192]{1,0:T(8,128)(2,1)}) fusion(f32[256,8192]{1,0:T(8,128)} %fusion.115, f32[256,8192]{1,0:T(8,128)} %fusion.116, bf16[8192,2048]{1,0:T(8,128)(2,1)} %all-gather.27.cloned.1.call-done, bf16[1,256,2048]{2,1,0:T(8,128)(2,1)} %param.27), kind=kOutput, calls=%fused_computation.74 | convolution fusion | flops 8623489024 | bytes 63963136 | tf_op jit(solution)/shard_map/dot_general | solution.py:23
  747.0 19.3 multiply_reduce_fusion
  774.2 93.1 %while.31 = (s32[]{:T(128)}, f32[8,1,256,4,64]{2,4,3,1,0:T(8,128)}, bf16[8,1,1024,64]{2,3,1,0:T(8,128)(2,1)}, bf16[8,1,1024,64]{2,3,1,0:T(8,128)(2,1)}, bf16[8,1...) while((s32[]{:T(128)}, f32[8,1,256,4,64]{2,4,3,1,0:T(8,128)}, ...), condition=%wide.region_9.10_spmd.clone.clone, body=%wide.region_7.9_spmd.clone.sunk.clone | while | flops 687209472 | bytes 34248824 | solution.py:158
  868.1 24.1 %reduce-scatter.10.cloned.1.call-done = bf16[1,256,512]{1,2,0:T(8,128)(2,1)} async-done(((bf16[1,1024,512]{1,2,0:T(8,128)(2,1)}), bf16[1,256,512]{1,2,0:T(8,128)(2,1)}) %reduce-scatter.10.cloned.1.call-update) | async-done | bytes 262160 | tf_op jit(solution)/shard_map/reduce_scatter | solution.py:280
  895.6 24.0 %reduce-scatter.12.cloned.1.call-done = bf16[1,256,512]{1,2,0:T(8,128)(2,1)} async-done(((bf16[1,1024,512]{1,2,0:T(8,128)(2,1)}), bf16[1,256,512]{1,2,0:T(8,128)(2,1)}) %reduce-scatter.12.cloned.1.call-update) | async-done | bytes 262160 | tf_op jit(solution)/shard_map/reduce_scatter | solution.py:283
  955.3 16.4 convolution_convert_fusion.1
  971.8 16.9 convolution_convert_fusion
  989.0 19.9 reduce-scatter.18.cloned.1.call-done
  1008.9 75.4 %reduce-scatter.14.cloned.1.call-done = bf16[256,2048]{1,0:T(8,128)(2,1)} async-done(((bf16[2048,2048]{1,0:T(8,128)(2,1)}), bf16[256,2048]{1,0:T(8,128)(2,1)}) %reduce-scatter.14.cloned.1.call-update) | async-done | bytes 1048592 | tf_op jit(solution)/shard_map/reduce_scatter | solution.py:308
  1084.4 75.4 %reduce-scatter.20.cloned.1.call-done = bf16[256,2048]{1,0:T(8,128)(2,1)} async-done(((bf16[2048,2048]{1,0:T(8,128)(2,1)}), bf16[256,2048]{1,0:T(8,128)(2,1)}) %reduce-scatter.20.cloned.1.call-update) | async-done | bytes 1048592 | tf_op jit(solution)/shard_map/reduce_scatter | solution.py:317
  1159.8 208.9 %reduce-scatter.22.cloned.1.call-done = bf16[256,8192]{1,0:T(8,128)(2,1)} async-done(((bf16[2048,8192]{1,0:T(8,128)(2,1)}), bf16[256,8192]{1,0:T(8,128)(2,1)}) %reduce-scatter.22.cloned.1.call-update) | async-done | bytes 4194320 | tf_op jit(solution)/shard_map/reduce_scatter | solution.py:168
  1368.7 209.0 %reduce-scatter.24.cloned.1.call-done = bf16[256,8192]{1,0:T(8,128)(2,1)} async-done(((bf16[2048,8192]{1,0:T(8,128)(2,1)}), bf16[256,8192]{1,0:T(8,128)(2,1)}) %reduce-scatter.24.cloned.1.call-update) | async-done | bytes 4194320 | tf_op jit(solution)/shard_map/reduce_scatter | solution.py:168
  1577.6 208.9 %reduce-scatter.26.cloned.1.call-done = bf16[1024,2048]{1,0:T(8,128)(2,1)} async-done(((bf16[8192,2048]{1,0:T(8,128)(2,1)}), bf16[1024,2048]{1,0:T(8,128)(2,1)}) %reduce-scatter.26.cloned.1.call-update) | async-done | bytes 4194320 | tf_op jit(solution)/shard_map/reduce_scatter | solution.py:168
  1796.1 17.7 fusion.78
  1850.2 450.8 %all-reduce.7.cloned.1.call-done = (bf16[256,2048]{1,0:T(8,128)(2,1)}, bf16[256,512]{1,0:T(8,128)(2,1)}, bf16[256,512]{1,0:T(8,128)(2,1)}, bf16[256,2048]{1,0:T(...) async-done(((bf16[256,2048]{1,0:T(8,128)(2,1)}, bf16[256,512]{1,0:T(8,128)(2,1)}, bf16[256,512]{1,0:T(8,128)(2,1)}, ...) | async-done | bytes 15204368 | tf_op jit(solution)/shard_map/psum | solution.py:329
  (267 shorter events, 345.1 us)
Async XLA Ops:
  7.2 33.2 %all-gather.13.cloned.1.call-start = ((), (), s32[]{:S(2)}) async-start(), calls=%async_computation.9 | async-start | bytes 2359296 | tf_op jit(solution)/shard_map/all_gather | solution.py:199
  7.9 62.2 %all-gather.15.cloned.1.call-start = ((), (), s32[]{:S(2)}) async-start(), calls=%async_computation.10 | async-start | bytes 2359296 | tf_op jit(solution)/shard_map/all_gather | solution.py:198
  8.7 80.4 %all-gather.29.cloned.1.call-start = ((), (), s32[]{:S(2)}) async-start(), calls=%async_computation.26 | async-start | bytes 1310720 | tf_op jit(solution)/shard_map/all_gather | solution.py:219
  19.8 137.5 %copy-start.17 = (f32[8,1,256]{2,1,0:T(1,128)}, f32[8,1,256]{2,1,0:T(1,128)S(1)}, u32[]{:S(2)}) copy-start(f32[8,1,256]{2,1,0:T(1,128)S(1)} %convert_element_type.290) | copy-start | bytes 24580
  21.3 136.0 %copy-start.21 = (f32[256]{0:T(256)}, f32[256]{0:T(256)S(1)}, u32[]{:S(2)}) copy-start(f32[256]{0:T(256)S(1)} %add_rsqrt_fusion.1) | copy-start | bytes 3076
  43.9 101.2 %all-gather.19.cloned.1.call-start = ((), (), s32[]{:S(2)}) async-start(), calls=%async_computation.12 | async-start | bytes 9437184 | tf_op jit(solution)/shard_map/all_gather | solution.py:197
  44.5 119.4 %all-gather.17.cloned.1.call-start = ((), (), s32[]{:S(2)}) async-start(), calls=%async_computation.11 | async-start | bytes 1310720 | tf_op jit(solution)/shard_map/all_gather | solution.py:213
  74.7 145.2 %all-gather.21.cloned.1.call-start = ((), (), s32[]{:S(2)}) async-start(), calls=%async_computation.13 | async-start | bytes 9437184 | tf_op jit(solution)/shard_map/all_gather | solution.py:200
  75.3 307.2 %all-gather.23.cloned.1.call-start = ((), (), s32[]{:S(2)}) async-start(), calls=%async_computation.14 | async-start | bytes 37748736 | tf_op jit(solution)/shard_map/all_gather | solution.py:229
  76.0 469.0 %all-gather.25.cloned.1.call-start = ((), (), s32[]{:S(2)}) async-start(), calls=%async_computation.15 | async-start | bytes 37748736 | tf_op jit(solution)/shard_map/all_gather | solution.py:230
  76.8 630.9 %all-gather.27.cloned.1.call-start = ((), (), s32[]{:S(2)}) async-start(), calls=%async_computation.16 | async-start | bytes 37748736 | tf_op jit(solution)/shard_map/all_gather | solution.py:231
  77.5 814.7 %reduce-scatter.10.cloned.1.call-start = ((), (), s32[]{:S(2)}) async-start(), calls=%async_computation.17 | async-start | bytes 1310720 | tf_op jit(solution)/shard_map/reduce_scatter | solution.py:280
  226.1 520.9 %copy-start.2 = (f32[256,2048]{1,0:T(8,128)}, f32[256,2048]{1,0:T(8,128)S(1)}, u32[]{:S(2)}) copy-start(f32[256,2048]{1,0:T(8,128)S(1)} %get-tuple-element.264) | copy-start | bytes 6291460
  226.4 318.7 %copy-start.5 = (bf16[256,2048]{1,0:T(8,128)(2,1)}, bf16[256,2048]{1,0:T(8,128)(2,1)S(1)}, u32[]{:S(2)}) copy-start(bf16[256,2048]{1,0:T(8,128)(2,1)S(1)} %multiply_convert_fusion.3) | copy-start | bytes 3145732
  774.2 119.0 %copy-start.16 = (f32[256,32]{0,1:T(8,128)S(1)}, f32[256,32]{0,1:T(8,128)}, u32[]{:S(2)}) copy-start(f32[256,32]{0,1:T(8,128)} %copy-done.15) | copy-start | bytes 98308
  867.3 52.3 %reduce-scatter.12.cloned.1.call-start = ((), (), s32[]{:S(2)}) async-start(), calls=%async_computation.18 | async-start | bytes 1310720 | tf_op jit(solution)/shard_map/reduce_scatter | solution.py:283
  868.1 121.0 %reduce-scatter.16.cloned.1.call-start = ((), (), s32[]{:S(2)}) async-start(), calls=%async_computation.20 | async-start | bytes 2359296 | tf_op jit(solution)/shard_map/reduce_scatter | solution.py:311
  895.6 113.3 %reduce-scatter.18.cloned.1.call-start = ((), (), s32[]{:S(2)}) async-start(), calls=%async_computation.21 | async-start | bytes 2359296 | tf_op jit(solution)/shard_map/reduce_scatter | solution.py:314
  922.7 161.6 %reduce-scatter.14.cloned.1.call-start = ((), (), s32[]{:S(2)}) async-start(), calls=%async_computation.19 | async-start | bytes 9437184 | tf_op jit(solution)/shard_map/reduce_scatter | solution.py:308
  931.8 227.9 %reduce-scatter.20.cloned.1.call-start = ((), (), s32[]{:S(2)}) async-start(), calls=%async_computation.22 | async-start | bytes 9437184 | tf_op jit(solution)/shard_map/reduce_scatter | solution.py:317
  939.0 429.7 %reduce-scatter.22.cloned.1.call-start = ((), (), s32[]{:S(2)}) async-start(), calls=%async_computation.23 | async-start | bytes 37748736 | tf_op jit(solution)/shard_map/reduce_scatter | solution.py:168
  955.3 622.3 %reduce-scatter.24.cloned.1.call-start = ((), (), s32[]{:S(2)}) async-start(), calls=%async_computation.24 | async-start | bytes 37748736 | tf_op jit(solution)/shard_map/reduce_scatter | solution.py:168
  971.8 814.8 %reduce-scatter.26.cloned.1.call-start = ((), (), s32[]{:S(2)}) async-start(), calls=%async_computation.25 | async-start | bytes 37748736 | tf_op jit(solution)/shard_map/reduce_scatter | solution.py:168
  988.8 1312.3 %all-reduce.7.cloned.1.call-start = ((), (), s32[]{:S(2)}) async-start(), calls=%async_computation.27 | async-start | bytes 30408704 | tf_op jit(solution)/shard_map/psum | solution.py:329
  (23 other events, 534.3 us)
Sparse Core Ops, SparseCore 0:
  9.9 30.4 all-gather.12
  42.3 27.7 all-gather.14
  72.3 16.7 all-gather.28
  90.8 54.2 all-gather.18
  147.0 16.8 all-gather.16
  165.6 54.2 all-gather.20
  221.8 160.6 all-gather.22
  384.4 160.6 all-gather.24
  547.0 160.6 all-gather.26
  867.4 24.7 reduce-scatter.9
  894.8 24.7 reduce-scatter.11
  923.3 41.1 reduce-scatter.15
  967.8 41.0 reduce-scatter.17
  1012.8 71.5 reduce-scatter.13
  1088.2 71.4 reduce-scatter.19
  1163.2 205.4 reduce-scatter.21
  1372.1 205.4 reduce-scatter.23
  1581.0 205.4 reduce-scatter.25
  1790.0 511.0 all-reduce.6
where the time goes:
time: 2340 us; the launch traced here: 2330 us
  waiting for transfers between devices  1860 us (79%)
  matrix products  330 us (14%)
  other arithmetic  57.3 us (2%)
  blocking collectives  46.1 us (2%)
    reduce_scatter x3, waiting for transfers between devices, scatter_rows(): lax.psum_scatter(dot_inner(left_rows, right_rows).astype(jnp.bfloat16), (...  627 us
    psum x1, waiting for transfers between devices, per_device(): lax.psum(query_share.astype(jnp.bfloat16), 'rep').astype(jnp.float32)  451 us
    all_gather x1, waiting for transfers between devices, per_device(): lax.all_gather(w_gate, ('dp', 'cp'), axis=0, tiled=True)  156 us
    all_gather x1, waiting for transfers between devices, per_device(): lax.all_gather(w_up, ('dp', 'cp'), axis=0, tiled=True)  142 us
    all_gather x1, waiting for transfers between devices, per_device(): lax.all_gather(w_down, ('dp', 'cp'), axis=0, tiled=True)  142 us
    reduce_scatter x1, waiting for transfers between devices, per_device(): lax.psum_scatter(query_w_grad.astype(jnp.bfloat16), ('dp', 'cp'), scatter...  75.4 us
    reduce_scatter x1, waiting for transfers between devices, per_device(): lax.psum_scatter(out_proj_grad.astype(jnp.bfloat16), ('dp', 'cp'), scatte...  75.4 us
    dot_general x7, matrix products, dot_back(): lax.dot_general(left_rows, right_rows, (((1,), (1,)), ((), ())), preferre...  74.7 us
  transfers between devices with their start and end apart: 19, of which 18 were waited for; matrix products, arithmetic and copies ran while one was open for 10% of the time, Pallas kernels for 0%

commit v1 on v0

v1 whole, which is shorter than its diff:
```python
import jax
import jax.numpy as jnp
from jax import lax
from jax.sharding import PartitionSpec as P

QUERY_HEADS = 32
KEY_VALUE_HEADS = 8
HEAD_SIZE = 64
NORM_EPS = 1e-05
ROPE_THETA = 500000.0
NEG_FILL = -1e30
GROUP = ("dp", "cp")
BF = jnp.bfloat16
F32 = jnp.float32


def matmul(left, right):
    return jnp.dot(left, right, preferred_element_type=F32)


def matmul_nt(left, right):
    return lax.dot_general(left, right, (((1,), (1,)), ((), ())), preferred_element_type=F32)


def matmul_tn(left, right):
    return lax.dot_general(left, right, (((0,), (0,)), ((), ())), preferred_element_type=F32)


def angle_tables(position_rows):
    inverse_freq = ROPE_THETA ** (-jnp.arange(HEAD_SIZE // 2, dtype=F32) * 2.0 / HEAD_SIZE)
    angle_table = position_rows.astype(F32)[:, None] * inverse_freq[None, :]
    return (jnp.cos(angle_table), jnp.sin(angle_table))


def apply_rotary(field_in, cosine_table, sine_values):
    shaped = field_in.reshape(field_in.shape[0], -1, HEAD_SIZE)
    leading = shaped[..., : HEAD_SIZE // 2]
    trailing = shaped[..., HEAD_SIZE // 2 :]
    cos_part = cosine_table[:, None, :]
    sin_part = sine_values[:, None, :]
    joined = jnp.concatenate(
        [leading * cos_part - trailing * sin_part, trailing * cos_part + leading * sin_part],
        axis=-1,
    )
    return joined.reshape(field_in.shape)


def inverse_rms(rows):
    return lax.rsqrt(jnp.mean(rows * rows, axis=-1, keepdims=True) + NORM_EPS)


def rms_back(rows, inverse, gain, grad_rows):
    scaled = grad_rows * gain
    gain_grad = jnp.sum(grad_rows * rows * inverse, axis=0)
    row_inner = jnp.mean(scaled * rows, axis=-1, keepdims=True)
    return (inverse * scaled - rows * inverse * inverse * inverse * row_inner, gain_grad)


def gather(rows):
    return lax.all_gather(rows, GROUP, axis=0, tiled=True)


def scatter(rows):
    return lax.psum_scatter(rows.astype(BF), GROUP, scatter_dimension=0, tiled=True)


def per_device(
    block_in,
    positions,
    norm_attn,
    w_query,
    key_weight,
    w_value,
    w_out,
    norm_ffn,
    w_gate,
    w_up,
    w_down,
    cotangent,
):
    dp = lax.axis_size("dp")
    cp = lax.axis_size("cp")
    n = dp * cp
    tokens, model = block_in.shape[1:]
    length = tokens * cp
    q_heads = QUERY_HEADS // n
    share = max(1, n // KEY_VALUE_HEADS)
    kv_heads = KEY_VALUE_HEADS * share // n
    group = q_heads // kv_heads
    qw, kw = q_heads * HEAD_SIZE, kv_heads * HEAD_SIZE

    x_own = block_in.reshape(tokens, model)
    g_own = cotangent.reshape(tokens, model)
    gain_attn = gather(norm_attn).astype(F32)
    gain_ffn = gather(norm_ffn).astype(F32)
    positions_all = lax.all_gather(positions, "dp", axis=0, tiled=True)
    x_all = gather(x_own)

    def to_columns(weight):
        rows, columns = weight.shape
        return lax.all_to_all(
            weight.reshape(rows, n, columns // n), GROUP, split_axis=1, concat_axis=0, tiled=True
        ).reshape(rows * n, columns // n)

    def to_rows(grad):
        rows, columns = grad.shape
        return lax.all_to_all(
            grad.astype(BF).reshape(rows, 1, columns), GROUP, split_axis=0, concat_axis=1, tiled=True
        ).reshape(rows // n, n * columns)

    rows = w_query.shape[0]

    def spread(weight):
        heads = weight.reshape(rows, KEY_VALUE_HEADS // kv_heads, kw)
        return jnp.repeat(heads, share, axis=1) if share > 1 else heads

    qkv_weight = jnp.concatenate(
        [w_query.reshape(rows, n, qw), spread(key_weight), spread(w_value)], axis=2
    ).reshape(rows, n * (qw + 2 * kw))
    qkv_columns = to_columns(qkv_weight)
    gate_columns = to_columns(w_gate)
    up_columns = to_columns(w_up)

    x_rows = x_all.astype(F32)
    normalized = (x_rows * inverse_rms(x_rows) * gain_attn).astype(BF)
    qkv = matmul(normalized, qkv_columns)
    cosine, sine = angle_tables(positions_all.reshape(-1))
    q = apply_rotary(qkv[:, :qw], cosine, sine).astype(BF)
    k = apply_rotary(qkv[:, qw : qw + kw], cosine, sine).astype(BF)
    v = qkv[:, qw + kw :].astype(BF)
    g_all = gather(g_own)

    def heads_of(x_, heads):
        return x_.reshape(dp, length, kv_heads, heads, HEAD_SIZE)

    allowed = positions_all[:, None, :] <= positions_all[:, :, None]

    def probs_of(q_one, k_one, ok):
        scores = (
            jnp.einsum("tkgd,lkd->kgtl", q_one, k_one, preferred_element_type=F32)
            * HEAD_SIZE ** (-0.5)
        )
        scores = jnp.where(ok, scores, NEG_FILL)
        weights = jnp.exp(scores - jnp.max(scores, axis=-1, keepdims=True))
        return weights / jnp.sum(weights, axis=-1, keepdims=True)

    def attend(operands):
        q_one, k_one, v_one, ok = operands
        probs = probs_of(q_one, k_one, ok).astype(BF)
        return jnp.einsum("kgtl,lkd->tkgd", probs, v_one, preferred_element_type=F32).astype(BF)

    q5, k4, v4 = heads_of(q, group), heads_of(k, 1)[..., 0, :], heads_of(v, 1)[..., 0, :]
    attended = lax.map(attend, (q5, k4, v4, allowed)).reshape(dp * length, qw)
    mid_own = x_own.astype(F32) + scatter(matmul(attended, w_out)).astype(F32)
    inverse_ffn = inverse_rms(mid_own)
    b_own = (mid_own * inverse_ffn * gain_ffn).astype(BF)
    b_all = gather(b_own)
    gate = matmul(b_all, gate_columns)
    up = matmul(b_all, up_columns)
    sigmoid = jax.nn.sigmoid(gate)
    hidden = (gate * sigmoid * up).astype(BF)
    hidden_grad = matmul_nt(g_all, w_down)
    gate_low = (hidden_grad * up * sigmoid * (1.0 + gate * (1.0 - sigmoid))).astype(BF)
    up_low = (hidden_grad * gate * sigmoid).astype(BF)
    ffn_in_grad = scatter(matmul_nt(gate_low, gate_columns) + matmul_nt(up_low, up_columns)).astype(F32)
    down_grad = matmul_tn(hidden, g_all).astype(BF)
    gate_grad = to_rows(matmul_tn(b_all, gate_low))
    up_grad = to_rows(matmul_tn(b_all, up_low))
    block_out = (mid_own + scatter(matmul(hidden, w_down)).astype(F32)).astype(BF)
    mid_part, gain_ffn_grad = rms_back(mid_own, inverse_ffn, gain_ffn, ffn_in_grad)
    mid_grad = g_own.astype(F32) + mid_part
    dr_all = gather(mid_grad.astype(BF))
    out_grad = matmul_tn(attended, dr_all).astype(BF)
    attended_grad = matmul_nt(dr_all, w_out).astype(BF)

    def attend_back(operands):
        q_one, k_one, v_one, ok, do_one = operands
        probs = probs_of(q_one, k_one, ok)
        low = probs.astype(BF)
        prob_grad = jnp.einsum("tkgd,lkd->kgtl", do_one, v_one, preferred_element_type=F32)
        inner = jnp.sum(probs * prob_grad, axis=-1, keepdims=True)
        score = (probs * (prob_grad - inner)).astype(BF)
        scale = HEAD_SIZE ** (-0.5)
        dq = jnp.einsum("kgtl,lkd->tkgd", score, k_one, preferred_element_type=F32) * scale
        dk = jnp.einsum("kgtl,tkgd->lkd", score, q_one, preferred_element_type=F32) * scale
        dv = jnp.einsum("kgtl,tkgd->lkd", low, do_one, preferred_element_type=F32)
        return dq, dk, dv

    dq, dk, dv = lax.map(attend_back, (q5, k4, v4, allowed, heads_of(attended_grad, group)))
    dqkv = jnp.concatenate(
        [
            apply_rotary(dq.reshape(dp * length, qw), cosine, -sine),
            apply_rotary(dk.reshape(dp * length, kw), cosine, -sine),
            dv.reshape(dp * length, kw),
        ],
        axis=1,
    ).astype(BF)
    qkv_grad = to_rows(matmul_tn(normalized, dqkv)).reshape(rows, n, qw + 2 * kw)
    normed_grad = scatter(matmul_nt(dqkv, qkv_columns)).astype(F32)
    in_own = x_own.astype(F32)
    in_part, gain_attn_grad = rms_back(in_own, inverse_rms(in_own), gain_attn, normed_grad)
    input_grad = (mid_grad + in_part).astype(BF)

    def fold(part):
        return part.reshape(rows, -1, share, kw).astype(F32).sum(axis=2).reshape(rows, -1)

    query_grad = qkv_grad[:, :, :qw].reshape(rows, n * qw)
    key_grad = fold(qkv_grad[:, :, qw : qw + kw])
    value_grad = fold(qkv_grad[:, :, qw + kw :])

    def over_rep(part):
        return lax.psum(part.astype(BF), "rep").astype(F32)

    return (
        block_out.reshape(block_in.shape),
        input_grad.reshape(block_in.shape),
        over_rep(scatter(gain_attn_grad)),
        over_rep(query_grad),
        over_rep(key_grad),
        over_rep(value_grad),
        over_rep(out_grad),
        over_rep(scatter(gain_ffn_grad)),
        over_rep(gate_grad),
        over_rep(up_grad),
        over_rep(down_grad),
    )


def solution(mesh):
    rows, both = P(("rep", "dp"), "cp", None), P(GROUP, None)
    return jax.shard_map(
        per_device,
        mesh=mesh,
        in_specs=(
            rows,
            P(("rep", "dp"), None),
            P(GROUP),
            both,
            both,
            both,
            both,
            P(GROUP),
            both,
            both,
            both,
            rows,
        ),
        out_specs=(rows, rows, P(GROUP), both, both, both, both, P(GROUP), both, both, both),
        check_vma=False,
    )
```

time: 2340 us -> 1570 us (0.67)
  waiting for transfers between devices: 1860 us -> 893 us
  local copies, waits for them, and re-layouts: 22.3 us -> 204 us
  matrix products: 330 us -> 243 us
  other arithmetic: 57.3 us -> 92.1 us
  blocking collectives: 46.1 us -> 77.4 us
  starting transfers between devices: 1.14 us -> 27.8 us
    reduce_scatter x9 -> x4, waiting for transfers between devices: 846 us -> 133 us  [scatter(): lax.psum_scatter(rows.astype(BF), GROUP, scatter_dimension=0, tiled=True)]
    all_gather x9 -> x4, waiting for transfers between devices: 556 us -> 73.6 us  [gather(): return lax.all_gather(rows, GROUP, axis=0, tiled=True)]
    all_to_all x0 -> x6, waiting for transfers between devices: none -> 213 us  [the longest x3 125 us: to_columns(): lax.all_to_all(weight.reshape(rows, n, columns // n), GROUP, split_axis=1...]
    unnamed x61 -> x113, local copies, waits for them, and re-layouts: 3.11 us -> 98.6 us
    dot_general x77 -> x29, matrix products: 330 us -> 243 us  [the longest x5 68.7 us: matmul_nt(): lax.dot_general(left, right, (((1,), (1,)), ((), ())), preferred_element_...]
    dynamic_update_slice x0 -> x8, local copies, waits for them, and re-layouts: none -> 44.2 us  [per_device(): lax.map(attend_back, (q5, k4, v4, allowed, heads_of(attended_grad, group)))]
    all_to_all x0 -> x5, local copies, waits for them, and re-layouts: none -> 27.9 us  [the longest x3 15 us: to_columns(): lax.all_to_all(weight.reshape(rows, n, columns // n), GROUP, split_axis=1...]
    all_gather x2 -> x3, blocking collectives: 19.5 us -> 47.3 us  [the longest x2 42.9 us: gather(): return lax.all_gather(rows, GROUP, axis=0, tiled=True)]
  transfers between devices with their start and end apart: 19 -> 15, of which waited for: 18 -> 9; matrix products, arithmetic and copies ran while one was open for 10% -> 15% of each run, Pallas kernels for 0% -> 0%
where the time goes in v1:
time: 1570 us; the launch traced here: 1550 us
  waiting for transfers between devices  893 us (57%)
  matrix products  243 us (15%)
  local copies, waits for them, and re-layouts  204 us (13%)
  other arithmetic  92.1 us (6%)
  blocking collectives  77.4 us (5%)
  starting transfers between devices  27.8 us (2%)
    psum x1, waiting for transfers between devices, over_rep(): return lax.psum(part.astype(BF), 'rep').astype(F32)  473 us
    reduce_scatter x4, waiting for transfers between devices, scatter(): lax.psum_scatter(rows.astype(BF), GROUP, scatter_dimension=0, tiled=True)  133 us
    all_to_all x3, waiting for transfers between devices, to_columns(): lax.all_to_all(weight.reshape(rows, n, columns // n), GROUP, split_axis=1...  125 us
    unnamed x113, local copies, waits for them, and re-layouts  98.6 us
    all_to_all x3, waiting for transfers between devices, to_rows(): lax.all_to_all(grad.astype(BF).reshape(rows, 1, columns), GROUP, split_ax...  87.6 us
    all_gather x4, waiting for transfers between devices, gather(): return lax.all_gather(rows, GROUP, axis=0, tiled=True)  73.6 us
    dot_general x5, matrix products, matmul_nt(): lax.dot_general(left, right, (((1,), (1,)), ((), ())), preferred_element_...  68.7 us
    dot_general x5, matrix products, matmul_tn(): lax.dot_general(left, right, (((0,), (0,)), ((), ())), preferred_element_...  60.1 us
  transfers between devices with their start and end apart: 15, of which 9 were waited for; matrix products, arithmetic and copies ran while one was open for 15% of the time, Pallas kernels for 0%

profile of v1, /device:TPU:0, one launch (start us, length us, event | category | flops | bytes accessed | tf_op | source)
XLA Modules:
  0.0 1554.0 jit_solution(9054698293486576124)
XLA Ops:
  18.2 34.1 %all-gather.2 = bf16[8,1,256]{2,1,0:T(2,128)(2,1)S(1)} all-gather(bf16[1,1,256]{2,1,0:T(2,128)(2,1)S(1)} %reshape.446), channel_id=1, replica_groups=mesh['rep'=4,'dp'=2,'cp'=4] {'dp','cp'}, dimensions={0}, use_global_device_ids=true | all-gather | bytes 4608 | tf_op jit(solution)/shard_map/all_gather | solution.py:60
  62.4 19.2 %all-gather.14.cloned.1.call-done = bf16[1,2048,2048]{2,1,0:T(8,128)(2,1)} async-done(((bf16[1,256,2048]{2,1,0:T(8,128)(2,1)}), bf16[1,2048,2048]{2,1,0:T(8,128)(2,1)}) %all-gather.14.cloned.1.call-update) | async-done | bytes 8388624 | tf_op jit(solution)/shard_map/all_gather | solution.py:60
  101.3 28.4 %while.24 = (s32[]{:T(128)}, bf16[2,1024,1,4,64]{1,4,3,2,0:T(8,128)(2,1)}, bf16[2,1024,1,64]{1,3,2,0:T(8,128)(2,1)}, pred[2,1024,1024]{1,2,0:T(8,128)(4,1)}, bf1...) while((s32[]{:T(128)}, bf16[2,1024,1,4,64]{1,4,3,2,0:T(8,128)(2,1)}, ...), condition=%wide.region_4.5_spmd, body=%wide.region_1.4_spmd.sunk | while | flops 1124327424 | bytes 66406572 | solution.py:153
  149.0 62.1 %reduce-scatter.5.cloned.1.call-done = bf16[256,2048]{1,0:T(8,128)(2,1)} async-done(((bf16[2048,2048]{1,0:T(8,128)(2,1)}), bf16[256,2048]{1,0:T(8,128)(2,1)}) %reduce-scatter.5.cloned.1.call-update) | async-done | bytes 1048592 | tf_op jit(solution)/shard_map/reduce_scatter | solution.py:64
  233.4 67.6 %all-to-all-done.1 = bf16[256,8,1024]{0,2,1:T(8,128)(2,1)} async-done(((bf16[256,8,1024]{0,2,1:T(8,128)(2,1)}), bf16[256,8,1024]{0,2,1:T(8,128)(2,1)}, u32[]{:S(2)}, u32[]{:S(2)}) %all-to-all-start.1) | async-done | bytes 4194336 | tf_op jit(solution)/shard_map/all_to_all | solution.py:101
  312.5 57.3 %all-to-all-done.2 = bf16[256,8,1024]{0,2,1:T(8,128)(2,1)} async-done(((bf16[256,8,1024]{0,2,1:T(8,128)(2,1)}), bf16[256,8,1024]{0,2,1:T(8,128)(2,1)}, u32[]{:S(2)}, u32[]{:S(2)}) %all-to-all-start.2) | async-done | bytes 4194336 | tf_op jit(solution)/shard_map/all_to_all | solution.py:101
  376.3 14.7 fusion.124
  402.0 23.3 %multiply_convert_fusion = (bf16[2048,1024]{1,0:T(8,128)(2,1)}, bf16[2048,1024]{1,0:T(8,128)(2,1)}, bf16[2048,1024]{1,0:T(8,128)(2,1)}) fusion(f32[2048,1024]{1,0:T(8,128)} %fusion.123, f32[2048,1024]{1,0:T(8,128)} %fusion.124, bf16[1024,2048]{1,0:T(8,128)(2,1)} %param.26, bf16[1,2048,2048]{2,1,0:T(8,128)(2,1)} %all-gather.16.cloned.1.call-done), kind=kOutput, calls=%fused_computation.77 | convolution fusion | flops 8623489024 | bytes 41943040 | tf_op jit(solution)/shard_map/dot_general | solution.py:22
  425.4 15.5 fusion.125
  440.9 16.2 %add_convert_fusion = bf16[2048,2048]{1,0:T(8,128)(2,1)} fusion(f32[2048,2048]{1,0:T(8,128)} %fusion.125, bf16[2048,1024]{1,0:T(8,128)(2,1)} %get-tuple-element.293, bf16[2048,1024]{1,0:T(8,128)(2,1)S(1)} %bitcast.385), kind=kOutput, calls=%fused_computation.72 | convolution fusion | flops 8598323200 | bytes 33554432 | tf_op jit(solution)/shard_map/dot_general | solution.py:22
  457.2 70.9 %reduce-scatter.9.cloned.1.call-done = bf16[256,2048]{1,0:T(8,128)(2,1)} async-done(((bf16[2048,2048]{1,0:T(8,128)(2,1)}), bf16[256,2048]{1,0:T(8,128)(2,1)}) %reduce-scatter.9.cloned.1.call-update) | async-done | bytes 1048592 | tf_op jit(solution)/shard_map/reduce_scatter | solution.py:64
  535.1 54.3 %all-gather.12.cloned.1.call-done = bf16[2048,2048]{1,0:T(8,128)(2,1)} async-done(((bf16[256,2048]{1,0:T(8,128)(2,1)}), bf16[2048,2048]{1,0:T(8,128)(2,1)}) %all-gather.12.cloned.1.call-update) | async-done | bytes 8388624 | tf_op jit(solution)/shard_map/all_gather | solution.py:60
  604.7 118.9 %while.25 = (s32[]{:T(128)}, f32[2,1024,1,4,64]{1,0,4,3,2:T(2,128)}, f32[2,1024,1,64]{1,0,3,2:T(2,128)}, bf16[2,1024,1,64]{1,3,2,0:T(8,128)(2,1)}, bf16[2,1024,1...) while((s32[]{:T(128)}, ...), condition=%wide.region_15.16_spmd, body=%wide.region_11.15_spmd.sunk | while | flops 2789527552 | bytes 167824624 | solution.py:189
  645.2 18.9 %dynamic_update_slice.23 = f32[2,1024,1,4,64]{1,0,4,3,2:T(2,128)} dynamic-update-slice(f32[2,1024,1,4,64]{1,0,4,3,2:T(2,128)} %get-tuple-element.450, f32[1,1024,1,4,64]{1,0,4,3,2:T(1,128)S(1)} %copy.231, s32[]{:T(128)S(6)} %copy.247, s32[]{:T(128)} %constant.67.clone.1..sunk, s32[]{:T(128)} %constant.67.clone.1..sunk, s32[]{:T(128)} %constant.67.clone.1..sunk, s32[]{:T(128)} %constant.67.clone.1..sunk) | dynamic-update-slice | bytes 2097156 | tf_op jit(solution)/shard_map/while/body/jit(dynamic_update_index_in_dim)/dynamic_update_slice | solution.py:189
  704.4 18.9 %dynamic_update_slice.23 = f32[2,1024,1,4,64]{1,0,4,3,2:T(2,128)} dynamic-update-slice(f32[2,1024,1,4,64]{1,0,4,3,2:T(2,128)} %get-tuple-element.450, f32[1,1024,1,4,64]{1,0,4,3,2:T(1,128)S(1)} %copy.231, s32[]{:T(128)S(6)} %copy.247, s32[]{:T(128)} %constant.67.clone.1..sunk, s32[]{:T(128)} %constant.67.clone.1..sunk, s32[]{:T(128)} %constant.67.clone.1..sunk, s32[]{:T(128)} %constant.67.clone.1..sunk) | dynamic-update-slice | bytes 2097156 | tf_op jit(solution)/shard_map/while/body/jit(dynamic_update_index_in_dim)/dynamic_update_slice | solution.py:189
  739.9 14.1 convolution_convert_fusion.1
  754.1 14.6 convert_bitcast_fusion
  789.4 14.1 convert_bitcast_fusion.1
  818.7 31.0 %all-to-all-done.5 = bf16[8,2,131072]{2,1,0:T(2,128)(2,1)} async-done(((bf16[8,2,131072]{2,1,0:T(2,128)(2,1)}), bf16[8,2,131072]{2,1,0:T(2,128)(2,1)}, u32[]{:S(2)}, u32[]{:S(2)}) %all-to-all-start.5) | async-done | bytes 4194336 | tf_op jit(solution)/shard_map/all_to_all | solution.py:107
  869.2 56.6 %all-to-all-done.4 = bf16[8,2,131072]{2,1,0:T(2,128)(2,1)} async-done(((bf16[8,2,131072]{2,1,0:T(2,128)(2,1)}), bf16[8,2,131072]{2,1,0:T(2,128)(2,1)}, u32[]{:S(2)}, u32[]{:S(2)}) %all-to-all-start.4) | async-done | bytes 4194336 | tf_op jit(solution)/shard_map/all_to_all | solution.py:107
  929.5 15.0 fusion.74
  1009.4 14.9 all-reduce.2
  1024.5 15.2 all-reduce.3
  1045.3 473.0 %all-reduce.7.cloned.1.call-done = (bf16[256,2048]{0,1:T(8,128)(2,1)}, bf16[256,512]{0,1:T(8,128)(2,1)}, bf16[256,512]{0,1:T(8,128)(2,1)}, bf16[256,8192]{0,1:T(...) async-done(((bf16[256,2048]{0,1:T(8,128)(2,1)}, bf16[256,512]{0,1:T(8,128)(2,1)}, bf16[256,512]{0,1:T(8,128)(2,1)}, ...) | async-done | bytes 15204368 | tf_op jit(solution)/shard_map/psum | solution.py:212
  (269 shorter events, 415.6 us)
Async XLA Ops:
  7.2 126.4 %copy-start = (bf16[256,2048]{1,0:T(8,128)(2,1)S(1)}, bf16[256,2048]{1,0:T(8,128)(2,1)}, u32[]{:S(2)}) copy-start(bf16[256,2048]{1,0:T(8,128)(2,1)} %param.22) | copy-start | bytes 3145732
  7.2 74.5 %all-gather.14.cloned.1.call-start = ((), (), s32[]{:S(2)}) async-start(), calls=%async_computation.16 | async-start | bytes 9437184 | tf_op jit(solution)/shard_map/all_gather | solution.py:60
  10.1 42.1 %copy-start.44 = (s32[1,1024]{1,0:T(1,128)S(1)}, s32[1,1024]{1,0:T(1,128)}, u32[]{:S(2)}) copy-start(s32[1,1024]{1,0:T(1,128)} %param.17) | copy-start | bytes 12292
  12.9 47.9 %all-to-all-start = ((bf16[256,8,384]{0,2,1:T(8,128)(2,1)}), bf16[256,8,384]{0,2,1:T(8,128)(2,1)S(1)}, u32[]{:S(2)}, u32[]{:S(2)}) async-start(bf16[256,8,384]{0,2,1:T(8,128)(2,1)} %pad_maximum_fusion), calls=%async_computation | async-start | bytes 3145728 | tf_op jit(solution)/shard_map/all_to_all | solution.py:101
  18.1 193.0 %reduce-scatter.5.cloned.1.call-start = ((), (), s32[]{:S(2)}) async-start(), calls=%async_computation.10 | async-start | bytes 9437184 | tf_op jit(solution)/shard_map/reduce_scatter | solution.py:64
  56.6 40.0 %copy-start.30 = (f32[1,8,2,128]{3,1,2,0:T(8,128)}, f32[1,8,2,128]{3,1,2,0:T(8,128)S(1)}, u32[]{:S(2)}) copy-start(f32[1,8,2,128]{3,1,2,0:T(8,128)S(1)} %copy.225) | copy-start | bytes 24580
  139.4 71.7 %copy-start.2 = (bf16[1,256,2048]{2,1,0:T(8,128)(2,1)S(1)}, bf16[1,256,2048]{2,1,0:T(8,128)(2,1)}, u32[]{:S(2)}) copy-start(bf16[1,256,2048]{2,1,0:T(8,128)(2,1)} %param.16) | copy-start | bytes 3145732
  139.5 236.8 %all-gather.10.cloned.1.call-start = ((), (), s32[]{:S(2)}) async-start(), calls=%async_computation.11 | async-start | bytes 9437184 | tf_op jit(solution)/shard_map/all_gather | solution.py:60
  149.0 381.9 %copy-start.28 = (f32[8,1,256]{2,1,0:T(1,128)}, f32[8,1,256]{2,1,0:T(1,128)S(1)}, u32[]{:S(2)}) copy-start(f32[8,1,256]{2,1,0:T(1,128)S(1)} %convert_element_type.227) | copy-start | bytes 24580
  212.8 318.1 %copy-start.34 = (f32[256]{0:T(256)}, f32[256]{0:T(256)S(1)}, u32[]{:S(2)}) copy-start(f32[256]{0:T(256)S(1)} %add_rsqrt_fusion.2) | copy-start | bytes 3076
  215.4 186.7 %all-gather.16.cloned.1.call-start = ((), (), s32[]{:S(2)}) async-start(), calls=%async_computation.17 | async-start | bytes 9437184 | tf_op jit(solution)/shard_map/all_gather | solution.py:60
  222.3 78.7 %all-to-all-start.1 = ((bf16[256,8,1024]{0,2,1:T(8,128)(2,1)}), bf16[256,8,1024]{0,2,1:T(8,128)(2,1)}, u32[]{:S(2)}, u32[]{:S(2)}) async-start(bf16[256,8,1024]{0,2,1:T(8,128)(2,1)} %bitcast.372), calls=%async_computation.2 | async-start | bytes 8388608 | tf_op jit(solution)/shard_map/all_to_all | solution.py:101
  301.0 68.8 %all-to-all-start.2 = ((bf16[256,8,1024]{0,2,1:T(8,128)(2,1)}), bf16[256,8,1024]{0,2,1:T(8,128)(2,1)}, u32[]{:S(2)}, u32[]{:S(2)}) async-start(bf16[256,8,1024]{0,2,1:T(8,128)(2,1)} %bitcast.371), calls=%async_computation.3 | async-start | bytes 8388608 | tf_op jit(solution)/shard_map/all_to_all | solution.py:101
  305.6 222.5 %reduce-scatter.9.cloned.1.call-start = ((), (), s32[]{:S(2)}) async-start(), calls=%async_computation.13 | async-start | bytes 9437184 | tf_op jit(solution)/shard_map/reduce_scatter | solution.py:64
  457.1 70.9 %copy-start.4 = (bf16[256,2048]{1,0:T(8,128)(2,1)S(1)}, bf16[256,2048]{1,0:T(8,128)(2,1)}, u32[]{:S(2)}) copy-start(bf16[256,2048]{1,0:T(8,128)(2,1)} %reduce-scatter.5.cloned.1.call-done) | copy-start | bytes 3145732
  457.2 132.3 %all-gather.12.cloned.1.call-start = ((), (), s32[]{:S(2)}) async-start(), calls=%async_computation.14 | async-start | bytes 9437184 | tf_op jit(solution)/shard_map/all_gather | solution.py:60
  535.1 472.5 %reduce-scatter.11.cloned.1.call-start = ((), (), s32[]{:S(2)}) async-start(), calls=%async_computation.15 | async-start | bytes 9437184 | tf_op jit(solution)/shard_map/reduce_scatter | solution.py:64
  604.7 122.5 %copy-start.31 = (f32[1,8,2,128]{3,1,2,0:T(8,128)S(1)}, f32[1,8,2,128]{3,1,2,0:T(8,128)}, u32[]{:S(2)}) copy-start(f32[1,8,2,128]{3,1,2,0:T(8,128)} %copy-done.30) | copy-start | bytes 24580
  604.7 122.5 %copy-start.42 = (f32[32]{0:T(128)S(1)}, f32[32]{0:T(128)}, u32[]{:S(2)}) copy-start(f32[32]{0:T(128)} %copy-done.41) | copy-start | bytes 388
  739.9 300.9 %reduce-scatter.7.cloned.1.call-start = ((), (), s32[]{:S(2)}) async-start(), calls=%async_computation.12 | async-start | bytes 9437184 | tf_op jit(solution)/shard_map/reduce_scatter | solution.py:64
  784.7 65.0 %all-to-all-start.5 = ((bf16[8,2,131072]{2,1,0:T(2,128)(2,1)}), bf16[8,2,131072]{2,1,0:T(2,128)(2,1)}, u32[]{:S(2)}, u32[]{:S(2)}) async-start(bf16[8,2,131072]{2,1,0:T(2,128)(2,1)} %reshape.467), calls=%async_computation.9 | async-start | bytes 8388608 | tf_op jit(solution)/shard_map/all_to_all | solution.py:107
  849.7 76.2 %all-to-all-start.4 = ((bf16[8,2,131072]{2,1,0:T(2,128)(2,1)}), bf16[8,2,131072]{2,1,0:T(2,128)(2,1)}, u32[]{:S(2)}, u32[]{:S(2)}) async-start(bf16[8,2,131072]{2,1,0:T(2,128)(2,1)} %reshape.465), calls=%async_computation.8 | async-start | bytes 8388608 | tf_op jit(solution)/shard_map/all_to_all | solution.py:107
  925.9 70.0 %all-to-all-start.3 = ((bf16[8,2,49152]{2,1,0:T(2,128)(2,1)}), bf16[8,2,49152]{2,1,0:T(2,128)(2,1)S(1)}, u32[]{:S(2)}, u32[]{:S(2)}) async-start(bf16[8,2,49152]{2,1,0:T(2,128)(2,1)} %reshape.463), calls=%async_computation.7 | async-start | bytes 3145728 | tf_op jit(solution)/shard_map/all_to_all | solution.py:107
  929.5 588.8 %all-reduce.7.cloned.1.call-start = ((), (), s32[]{:S(2)}) async-start(), calls=%async_computation.18 | async-start | bytes 30408704 | tf_op jit(solution)/shard_map/psum | solution.py:212
  (46 other events, 594.2 us)
Sparse Core Ops, SparseCore 0:
  9.9 71.7 all-gather.13
  139.6 71.4 reduce-scatter.4
  215.5 91.9 all-gather.9
  309.2 80.9 all-gather.15
  457.3 70.7 reduce-scatter.8
  535.2 54.2 all-gather.11
  740.0 94.0 reduce-scatter.10
  838.1 119.8 reduce-scatter.6
  1005.8 512.4 all-reduce.6
